TPU v7x, 32 devices: a whole 2x2x4 slice. The times are simulated.
32 devices in a mesh: parts: 2 (over y), row: 4 (over z), col: 4 (over x, core).
Axes of the slice: x: 2, y: 2, z: 4, core: 2. Of those that a mesh axis runs over, the one named last changes fastest.
Arguments:
- sigma_anc: float32 [24576, 12288], P(('parts', 'row'), 'col'), parts along dimension 0
- normal_factor: float32 [4, 12288, 512], P('parts', ('col', 'row')), parts along dimension 0, may hold values from -0.078125 to 0.078125
- jj_inverse: float32 [4, 512, 512], P('parts', None, 'col'), parts along dimension 0, may hold values from -6 to 6
- blocks: int32 [4, 128], P('parts'), parts along dimension 0, may hold values from 0 to 255, as said below
Outputs:
- sigma_rj: float32 [4, 12288, 512], P('parts', 'row', 'col'), parts along dimension 0
- sigma_jj: float32 [4, 512, 512], P('parts', None, 'col'), parts along dimension 0
There are 2 independent parts, one for each index of `parts`. A program takes and returns all parts, laid end to end along the dimension named above; each array names one. Nothing has to cross between parts.
Inputs may be any that keep to these rules, and one draw needn't show every extreme that they name: Each list names 128 different blocks and always holds block 0 and block 255.
All inputs are finite; a program needn't handle non-finite values.
Results may differ from a plain program's by a relative error of at most 0.0001.
Values sent between devices are 32-bit elements; how exact they have to be, the bound alone decides.
A program may use at most 192 MiB of HBM per device.

v0:
```python
import jax
import jax.numpy as jnp
from jax import lax
from jax.sharding import PartitionSpec as P

BLK = 48


def broadcast(value, axis, source):
    kept = jnp.where(lax.axis_index(axis) == source, value, 0).astype(value.dtype)
    return lax.psum(kept, axis)


def listed_mask(blocks, first_block, count, rows):
    block_ids = first_block + jnp.arange(count, dtype=jnp.int32)
    listed = jnp.any(blocks[:, :, None] == block_ids[None, None, :], axis=1).astype(jnp.float32)
    return jnp.repeat(listed, BLK, axis=1, total_repeat_length=rows)[:, :, None]


def shards(sigma_anc, normal_factor, jj_inverse, blocks):
    tile_rows, tile_cols = sigma_anc.shape
    row_count = lax.axis_size("row")
    row_index = lax.axis_index("row")
    col_index = lax.axis_index("col")
    local_rows = normal_factor.shape[1]
    local_blocks = local_rows // BLK
    first_local = (col_index * row_count + row_index) * local_blocks
    masked = normal_factor * listed_mask(blocks, first_local, local_blocks, local_rows)
    row_blocks = tile_rows // BLK
    row_mask = listed_mask(blocks, row_index * row_blocks, row_blocks, tile_rows)
    start_row = row_index * tile_rows
    root_col = start_row // tile_cols
    offset = jnp.clip(start_row - col_index * tile_cols, 0, tile_cols - tile_rows)
    partial_list = []
    slab_list = []
    for supernode in range(2):
        gathered = lax.all_gather(masked[supernode], "row", axis=0, tiled=True)
        partial_list.append(
            jnp.dot(
                sigma_anc,
                gathered,
                precision=lax.Precision.HIGHEST,
                preferred_element_type=jnp.float32,
            )
        )
        slab_list.append(lax.dynamic_slice_in_dim(gathered, offset, tile_rows, 0))
    partials = jnp.stack(partial_list)
    slabs = jnp.stack(slab_list)
    summed = lax.psum(partials, "col")
    full_rj = -(summed * row_mask)
    part_cols = jj_inverse.shape[2]
    sigma_rj = lax.dynamic_slice_in_dim(full_rj, col_index * part_cols, part_cols, 2)
    owner_rows = broadcast(slabs, "col", root_col)
    update = jnp.einsum("srw,srv->swv", owner_rows, sigma_rj, precision=lax.Precision.HIGHEST)
    sigma_jj = jj_inverse - lax.psum(update, "row")
    return (sigma_rj, sigma_jj)


def solution(mesh):
    placed = (
        P(("parts", "row"), "col"),
        P("parts", ("col", "row"), None),
        P("parts", None, "col"),
        P("parts", None),
    )
    return jax.shard_map(
        shards,
        mesh=mesh,
        in_specs=placed,
        out_specs=(P("parts", "row", "col"), P("parts", None, "col")),
        check_vma=False,
    )
```

profile of v0, /device:TPU:0, one launch (start us, length us, event | category | flops | bytes accessed | tf_op | source)
XLA Modules:
  0.0 816.3 jit_solution(12783318977597875389)
XLA Ops:
  7.2 0.0 all-gather.5.cloned.1.call-start
  7.2 0.9 compare_reduce_fusion.1
  8.1 0.1 copy.11
  8.2 0.7 pad_clamp_fusion
  8.9 1.6 gather_fusion
  10.5 0.1 copy.12
  10.6 2.4 copy.13
  13.0 0.2 broadcast_multiply_fusion
  13.2 1.9 fusion.11
  15.1 0.0 all-gather.5.cloned.1.call-update
  15.1 0.0 all-gather.7.cloned.1.call-start
  15.2 0.7 all-gather.7.cloned.1.call-update
  15.9 0.0 all-reduce.6.cloned.1.call-start
  16.0 117.4 %all-gather.5.cloned.1.call-done = f32[1,3072,512]{1,2,0:T(8,128)} async-done(((f32[1,768,512]{1,2,0:T(8,128)}), f32[1,3072,512]{1,2,0:T(8,128)}) %all-gather.5.cloned.1.call-update) | async-done | bytes 6291472 | tf_op jit(solution)/shard_map/all_gather | solution.py:37
  133.3 67.8 %fusion.4 = f32[1,3072,512]{1,2,0:T(8,128)} fusion(f32[3072,3072]{1,0:T(8,128)} %param.8, f32[1,3072,512]{1,2,0:T(8,128)} %all-gather.5.cloned.1.call-done), kind=kOutput, calls=%fused_computation.8 | convolution fusion | flops 57982058496 | bytes 50331648 | tf_op jit(solution)/shard_map/dot_general | solution.py:39
  201.1 47.4 %all-gather.7.cloned.1.call-done = f32[1,3072,512]{1,2,0:T(8,128)} async-done(((f32[1,768,512]{1,2,0:T(8,128)}), f32[1,3072,512]{1,2,0:T(8,128)}) %all-gather.7.cloned.1.call-update) | async-done | bytes 6291472 | tf_op jit(solution)/shard_map/all_gather | solution.py:37
  248.5 0.0 copy-start
  248.5 0.0 copy-start.1
  248.5 68.0 %fusion.7 = f32[1,3072,512]{1,2,0:T(8,128)} fusion(f32[3072,3072]{1,0:T(8,128)} %param.8, f32[1,3072,512]{1,2,0:T(8,128)} %all-gather.7.cloned.1.call-done), kind=kOutput, calls=%fused_computation.9 | convolution fusion | flops 57982058496 | bytes 50331648 | tf_op jit(solution)/shard_map/dot_general | solution.py:39
  316.5 0.0 copy-done
  316.5 0.0 copy-done.1
  316.5 14.6 %pad_maximum_fusion = (f32[2,3072,512]{1,2,0:T(8,128)}, f32[2,3072,512]{1,2,0:T(8,128)}) fusion(f32[1,3072,512]{1,2,0:T(8,128)} %fusion.7, f32[1,3072,512]{1,2,0:T(8,128)} %fusion.4, f32[1,3072,512]{1,2,0:T(8,128)S(1)} %copy-done.1, f32[1,3072,512]{1,2,0:T(8,128)S(1)} %copy-done, pred[]{:T(512)S(6)} %eq.35), kind=kLoop, calls=%fused_computation.2 | loop fusion | flops 9437184 | bytes 50331648 | tf_op jit(solution)/shard_map/stack | solution.py:47
  331.0 0.0 copy-start.3
  331.0 0.0 copy-start.2
  331.0 0.0 all-reduce.6.cloned.1.call-update
  331.0 0.0 all-reduce.4.cloned.1.call-start
  331.1 0.6 copy-done.3
  331.7 0.2 compare_reduce_fusion
  331.9 0.1 copy.14
  332.0 0.0 copy-done.2
  332.0 8.1 gather_fusion.1
  340.1 0.5 copy.15
  340.6 412.4 %all-reduce.6.cloned.1.call-done = (f32[2,3072,512]{1,2,0:T(8,128)}, f32[2,3072,512]{1,2,0:T(8,128)}) async-done(((f32[2,3072,512]{1,2,0:T(8,128)}, f32[2,3072,512]{1,2,0:T(8,128)}), (f32[2,3072,512]{1,2,0:T(8,128)}, f32[2,3072,512]{1,2,0:T(8,128)})) %all-reduce.6.cloned.1.call-update) | async-done | bytes 25165840 | tf_op jit(solution)/shard_map/psum | solution.py:49
  753.0 2.2 fusion.10
  755.2 13.8 %fusion.12 = f32[2,512,128]{2,1,0:T(8,128)} fusion(f32[2,3072,512]{1,2,0:T(8,128)} %get-tuple-element.31, f32[2,3072,128]{1,2,0:T(8,128)S(1)} %fusion.10), kind=kOutput, calls=%fused_computation.20 | convolution fusion | flops 4831838208 | bytes 16252928 | tf_op jit(solution)/shard_map/srw,srv->swv/dot_general | solution.py:54
  769.1 0.0 all-reduce.4.cloned.1.call-update
  769.1 2.4 copy.17
  771.4 36.3 %all-reduce.4.cloned.1.call-done = f32[2,512,128]{2,1,0:T(8,128)} async-done(((f32[2,512,128]{2,1,0:T(8,128)}), f32[2,512,128]{2,1,0:T(8,128)}) %all-reduce.4.cloned.1.call-update) | async-done | bytes 524304 | tf_op jit(solution)/shard_map/psum | solution.py:55
  807.7 2.0 sub.7
  (5 shorter events, 0.0 us)
Async XLA Ops:
  7.2 126.2 %all-gather.5.cloned.1.call-start = ((), (), s32[]{:S(2)}) async-start(), calls=%async_computation.1 | async-start | bytes 7864320 | tf_op jit(solution)/shard_map/all_gather | solution.py:37
  15.1 233.3 %all-gather.7.cloned.1.call-start = ((), (), s32[]{:S(2)}) async-start(), calls=%async_computation.2 | async-start | bytes 7864320 | tf_op jit(solution)/shard_map/all_gather | solution.py:37
  15.9 737.1 %all-reduce.6.cloned.1.call-start = ((), (), s32[]{:S(2)}) async-start(), calls=%async_computation.3 | async-start | bytes 50331648 | tf_op jit(solution)/shard_map/psum | solution.py:49
  248.5 68.0 %copy-start = (f32[1,3072,512]{1,2,0:T(8,128)S(1)}, f32[1,3072,512]{1,2,0:T(8,128)}, u32[]{:S(2)}) copy-start(f32[1,3072,512]{1,2,0:T(8,128)} %all-gather.5.cloned.1.call-done) | copy-start | bytes 18874372
  248.5 68.0 %copy-start.1 = (f32[1,3072,512]{1,2,0:T(8,128)S(1)}, f32[1,3072,512]{1,2,0:T(8,128)}, u32[]{:S(2)}) copy-start(f32[1,3072,512]{1,2,0:T(8,128)} %all-gather.7.cloned.1.call-done) | copy-start | bytes 18874372
  331.0 0.7 copy-start.3
  331.0 1.0 copy-start.2
  331.0 476.7 %all-reduce.4.cloned.1.call-start = ((), (), s32[]{:S(2)}) async-start(), calls=%async_computation | async-start | bytes 1048576 | tf_op jit(solution)/shard_map/psum | solution.py:55
Sparse Core Ops, SparseCore 0:
  15.3 118.0 all-gather.4
  134.9 113.5 all-gather.6
  331.2 421.7 all-reduce.5
  769.2 38.4 all-reduce.3
where the time goes:
time: 817 us; the launch traced here: 816 us
  waiting for transfers between devices  614 us (75%)
  matrix products  150 us (18%)
  other arithmetic  20.8 us (3%)
  local copies, waits for them, and re-layouts  17.7 us (2%)
  between operations  13.9 us (2%)
    psum x1, waiting for transfers between devices, shards(): summed = lax.psum(partials, 'col')  412 us
    all_gather x2, waiting for transfers between devices, shards(): gathered = lax.all_gather(masked[supernode], 'row', axis=0, tiled=True)  165 us
    dot_general x2, matrix products, shards(): jnp.dot(sigma_anc, gathered, precision=lax.Precision.HIGHEST, preferred_e...  136 us
    psum x1, waiting for transfers between devices, shards(): sigma_jj = jj_inverse - lax.psum(update, 'row')  36.3 us
  transfers between devices with their start and end apart: 4, of which 4 were waited for; matrix products, arithmetic and copies ran while one was open for 10% of the time, Pallas kernels for 0%

commit v1 on v0

--- a/solution.py
+++ b/solution.py
@@ -46,7 +46,9 @@
         slab_list.append(lax.dynamic_slice_in_dim(gathered, offset, tile_rows, 0))
     partials = jnp.stack(partial_list)
     slabs = jnp.stack(slab_list)
-    summed = lax.psum(partials, "col")
+    summed = partials
+    for hop in (1, 2):
+        summed = summed + lax.ppermute(summed, "col", [(dev, dev ^ hop) for dev in range(4)])
     full_rj = -(summed * row_mask)
     part_cols = jj_inverse.shape[2]
     sigma_rj = lax.dynamic_slice_in_dim(full_rj, col_index * part_cols, part_cols, 2)

time: 817 us -> 891 us (1.091)
  waiting for transfers between devices: 614 us -> 671 us
  other arithmetic: 20.8 us -> 36.3 us
    ppermute x0 -> x2, waiting for transfers between devices: none -> 472 us  [shards(): lax.ppermute(summed, 'col', [(dev, dev ^ hop) for dev in range(4)])]
    psum x1, waiting for transfers between devices: 412 us -> 0.02 us  [broadcast(): return lax.psum(kept, axis)]
    select_n x0 -> x1, other arithmetic: none -> 11.6 us  [broadcast(): jnp.where(lax.axis_index(axis) == source, value, 0).astype(value.dtype)]
  transfers between devices with their start and end apart: 4 -> 6, of which waited for: 4 -> 5; matrix products, arithmetic and copies ran while one was open for 10% -> 11% of each run, Pallas kernels for 0% -> 0%
where the time goes in v1:
time: 891 us; the launch traced here: 890 us
  waiting for transfers between devices  671 us (75%)
  matrix products  149 us (17%)
  other arithmetic  36.3 us (4%)
  local copies, waits for them, and re-layouts  17.7 us (2%)
  between operations  13.9 us (2%)
    ppermute x2, waiting for transfers between devices, shards(): lax.ppermute(summed, 'col', [(dev, dev ^ hop) for dev in range(4)])  472 us
    all_gather x2, waiting for transfers between devices, shards(): gathered = lax.all_gather(masked[supernode], 'row', axis=0, tiled=True)  165 us
    dot_general x2, matrix products, shards(): jnp.dot(sigma_anc, gathered, precision=lax.Precision.HIGHEST, preferred_e...  136 us
    psum x1, waiting for transfers between devices, shards(): sigma_jj = jj_inverse - lax.psum(update, 'row')  34.3 us
  transfers between devices with their start and end apart: 6, of which 5 were waited for; matrix products, arithmetic and copies ran while one was open for 11% of the time, Pallas kernels for 0%

profile of v1, /device:TPU:0, one launch (start us, length us, event | category | flops | bytes accessed | tf_op | source)
XLA Modules:
  0.0 890.4 jit_solution(11378581451474894549)
XLA Ops:
  7.2 0.0 all-gather.5.cloned.1.call-start
  7.2 0.9 compare_reduce_fusion.1
  8.1 0.1 copy.11
  8.2 0.7 pad_clamp_fusion
  8.9 1.6 gather_fusion
  10.5 0.1 copy.12
  10.6 2.4 copy.13
  13.0 0.2 broadcast_multiply_fusion
  13.2 1.9 fusion.13
  15.1 0.0 all-gather.5.cloned.1.call-update
  15.1 0.0 all-gather.7.cloned.1.call-start
  15.2 0.7 all-gather.7.cloned.1.call-update
  15.9 0.0 all-reduce.3.cloned.1.call-start
  15.9 117.4 %all-gather.5.cloned.1.call-done = f32[1,3072,512]{1,2,0:T(8,128)} async-done(((f32[1,768,512]{1,2,0:T(8,128)}), f32[1,3072,512]{1,2,0:T(8,128)}) %all-gather.5.cloned.1.call-update) | async-done | bytes 6291472 | tf_op jit(solution)/shard_map/all_gather | solution.py:37
  133.3 67.8 %fusion.4 = f32[1,3072,512]{1,2,0:T(8,128)} fusion(f32[3072,3072]{1,0:T(8,128)} %param.8, f32[1,3072,512]{1,2,0:T(8,128)} %all-gather.5.cloned.1.call-done), kind=kOutput, calls=%fused_computation.8 | convolution fusion | flops 57982058496 | bytes 50331648 | tf_op jit(solution)/shard_map/dot_general | solution.py:39
  201.1 47.4 %all-gather.7.cloned.1.call-done = f32[1,3072,512]{1,2,0:T(8,128)} async-done(((f32[1,768,512]{1,2,0:T(8,128)}), f32[1,3072,512]{1,2,0:T(8,128)}) %all-gather.7.cloned.1.call-update) | async-done | bytes 6291472 | tf_op jit(solution)/shard_map/all_gather | solution.py:37
  248.4 0.0 copy-start
  248.5 67.8 %fusion.7 = f32[1,3072,512]{1,2,0:T(8,128)} fusion(f32[3072,3072]{1,0:T(8,128)} %param.8, f32[1,3072,512]{1,2,0:T(8,128)} %all-gather.7.cloned.1.call-done), kind=kOutput, calls=%fused_computation.9 | convolution fusion | flops 57982058496 | bytes 50331648 | tf_op jit(solution)/shard_map/dot_general | solution.py:39
  316.3 0.0 copy-done
  316.3 8.6 pad_maximum_fusion
  324.9 0.1 collective-permute-start
  324.9 19.3 %collective-permute-done = f32[2,3072,512]{1,2,0:T(8,128)S(1)} collective-permute-done((f32[2,3072,512]{1,2,0:T(8,128)}, f32[2,3072,512]{1,2,0:T(8,128)S(1)}, u32[]{:S(2)}, u32[]{:S(2)}) %collective-permute-start) | collective-permute-done | bytes 12582944 | tf_op jit(solution)/shard_map/ppermute | solution.py:51
  344.2 8.8 fusion.12
  353.0 1.5 collective-permute-start.1
  354.4 11.6 %maximum_select_fusion = f32[2,3072,512]{1,2,0:T(8,128)} fusion(f32[1,3072,512]{1,2,0:T(8,128)} %all-gather.7.cloned.1.call-done, f32[1,3072,512]{1,2,0:T(8,128)} %all-gather.5.cloned.1.call-done, pred[]{:T(512)S(6)} %eq.35), kind=kLoop, calls=%fused_computation.3 | loop fusion | flops 6291456 | bytes 25165824 | tf_op jit(solution)/shard_map/jit(_where)/select_n | solution.py:10
  366.0 0.0 copy-start.2
  366.0 0.0 copy-start.1
  366.1 0.0 all-reduce.3.cloned.1.call-update
  366.1 0.0 all-reduce.5.cloned.1.call-start
  366.1 0.6 copy-done.2
  366.7 0.2 compare_reduce_fusion
  366.9 0.1 copy.14
  367.0 0.0 copy-done.1
  367.0 8.1 gather_fusion.1
  375.2 0.5 copy.15
  375.6 452.3 %collective-permute-done.1 = f32[2,3072,512]{1,2,0:T(8,128)} collective-permute-done((f32[2,3072,512]{1,2,0:T(8,128)}, f32[2,3072,512]{1,2,0:T(8,128)}, u32[]{:S(2)}, u32[]{:S(2)}) %collective-permute-start.1) | collective-permute-done | bytes 12582944 | tf_op jit(solution)/shard_map/ppermute | solution.py:51
  827.9 3.4 fusion.11
  831.3 0.0 all-reduce.3.cloned.1.call-done
  831.4 13.9 %fusion.14 = f32[2,512,128]{2,1,0:T(8,128)} fusion(f32[2,3072,512]{1,2,0:T(8,128)} %all-reduce.3.cloned.1.call-done, f32[2,3072,128]{1,2,0:T(8,128)S(1)} %fusion.11), kind=kOutput, calls=%fused_computation.22 | convolution fusion | flops 4831838208 | bytes 16252928 | tf_op jit(solution)/shard_map/srw,srv->swv/dot_general | solution.py:56
  845.2 0.0 all-reduce.5.cloned.1.call-update
  845.2 2.4 copy.17
  847.6 34.3 %all-reduce.5.cloned.1.call-done = f32[2,512,128]{2,1,0:T(8,128)} async-done(((f32[2,512,128]{2,1,0:T(8,128)}), f32[2,512,128]{2,1,0:T(8,128)}) %all-reduce.5.cloned.1.call-update) | async-done | bytes 524304 | tf_op jit(solution)/shard_map/psum | solution.py:57
  881.9 2.0 sub.7
  (5 shorter events, 0.0 us)
Async XLA Ops:
  7.2 126.1 %all-gather.5.cloned.1.call-start = ((), (), s32[]{:S(2)}) async-start(), calls=%async_computation.2 | async-start | bytes 7864320 | tf_op jit(solution)/shard_map/all_gather | solution.py:37
  15.1 233.3 %all-gather.7.cloned.1.call-start = ((), (), s32[]{:S(2)}) async-start(), calls=%async_computation.3 | async-start | bytes 7864320 | tf_op jit(solution)/shard_map/all_gather | solution.py:37
  15.9 815.5 %all-reduce.3.cloned.1.call-start = ((), (), s32[]{:S(2)}) async-start(), calls=%async_computation | async-start | bytes 25165824 | tf_op jit(solution)/shard_map/psum | solution.py:11
  248.4 67.8 %copy-start = (f32[1,3072,512]{1,2,0:T(8,128)S(1)}, f32[1,3072,512]{1,2,0:T(8,128)}, u32[]{:S(2)}) copy-start(f32[1,3072,512]{1,2,0:T(8,128)} %fusion.4) | copy-start | bytes 18874372
  324.9 19.4 %collective-permute-start = (f32[2,3072,512]{1,2,0:T(8,128)}, f32[2,3072,512]{1,2,0:T(8,128)S(1)}, u32[]{:S(2)}, u32[]{:S(2)}) collective-permute-start(f32[2,3072,512]{1,2,0:T(8,128)} %pad_maximum_fusion), channel_id=1, source_target_pairs={{0,1},{1,0},{2,3},{3,2},{4,5},{5,4},{6,7},{7,6},{8,9},{9,8},{10,11... | collective-permute-start | bytes 37748744 | tf_op jit(solution)/shard_map/ppermute | solution.py:51
  353.0 474.9 %collective-permute-start.1 = (f32[2,3072,512]{1,2,0:T(8,128)}, f32[2,3072,512]{1,2,0:T(8,128)}, u32[]{:S(2)}, u32[]{:S(2)}) collective-permute-start(f32[2,3072,512]{1,2,0:T(8,128)} %fusion.12), channel_id=1, source_target_pairs={{0,2},{1,3},{2,0},{3,1},{4,6},{5,7},{6,4},{7,5},{8,10},{9,11},{10,... | collective-permute-start | bytes 37748744 | tf_op jit(solution)/shard_map/ppermute | solution.py:51
  366.0 0.7 copy-start.2
  366.0 1.0 copy-start.1
  366.1 515.8 %all-reduce.5.cloned.1.call-start = ((), (), s32[]{:S(2)}) async-start(), calls=%async_computation.1 | async-start | bytes 1048576 | tf_op jit(solution)/shard_map/psum | solution.py:57
Sparse Core Ops, SparseCore 0:
  15.2 118.0 all-gather.4
  134.9 113.5 all-gather.6
  366.2 420.4 all-reduce.2
  845.3 36.4 all-reduce.4
